TPU v7x, 128 devices: a whole 4x4x4 slice. The times are simulated.
128 devices in a mesh: path: 16 (over x, z), fsdp: 8 (over y, core).
Axes of the slice: x: 4, y: 4, z: 4, core: 2. Of those that a mesh axis runs over, the one named last changes fastest.
Arguments:
- tokens: bfloat16 [16, 1024, 2048], P('path', 'fsdp'), may hold values from -6 to 6
- cotangent: bfloat16 [16, 1024, 2048], P('path', 'fsdp'), may hold values from -6 to 6
- norm_gain: float32 [16, 2, 2048], P('path'), may hold values from 0.1 to 1.9
- up_proj: bfloat16 [16, 2, 2048, 4096], P('path', None, None, 'fsdp'), as said below
- down_proj: bfloat16 [16, 2, 2048, 4096], P('path', None, None, 'fsdp'), as said below
- mom_up: float32 [8, 2048, 4096], P(None, 'path', 'fsdp'), may hold values from -4 to 4
- mom_down: float32 [8, 2048, 4096], P(None, 'path', 'fsdp'), may hold values from -4 to 4
- share_table: int32 [16, 2], replicated, may hold values from 0 to 3, as said below
- module_slot: int32 [8], replicated, may hold values from 0 to 7, each once
Outputs:
- new_up: bfloat16 [16, 2, 2048, 4096], P('path', None, None, 'fsdp')
- new_down: bfloat16 [16, 2, 2048, 4096], P('path', None, None, 'fsdp')
- new_mom_up: float32 [8, 2048, 4096], P(None, 'path', 'fsdp')
- new_mom_down: float32 [8, 2048, 4096], P(None, 'path', 'fsdp')
Inputs may be any that keep to these rules, and one draw needn't show every extreme that they name: share_table[p, l] is the index, within level l, of the module that path p uses; a module may be shared by several paths or by none. Copies of one module are equal: up_proj[p, l] equals up_proj[q, l] and down_proj[p, l] equals down_proj[q, l] whenever share_table[p, l] = share_table[q, l]. `down_proj`: copies of one module are equal, as for up_proj.
All inputs are finite; a program needn't handle non-finite values.
Results may differ from a plain program's by a relative error of at most 0.012.
Values may be sent and summed in bfloat16 or wider, within the bound.
A program may use at most 128 MiB of HBM per device.

v0:
```python
import math

import jax
import jax.numpy as jnp
from jax import lax
from jax.sharding import PartitionSpec as P

D = 2048
FF = 4096
PER_LEVEL = 4


epsilon = 1e-06
gelu_coef = 0.7978845608
cubic_coef = 0.044715
momentum_decay = 0.9
outer_rate = 0.7


def gelu_tanh(value):
    inner = gelu_coef * (value + cubic_coef * value * value * value)
    return 0.5 * value * (1.0 + jnp.tanh(inner))


def gelu_slope(value):
    inner = gelu_coef * (value + cubic_coef * value * value * value)
    tangent = jnp.tanh(inner)
    return 0.5 * (1.0 + tangent) + 0.5 * value * (1.0 - tangent * tangent) * gelu_coef * (
        1.0 + 3.0 * cubic_coef * value * value
    )


def rms_norm(rows, gain):
    return rows * lax.rsqrt(jnp.mean(rows * rows, axis=-1, keepdims=True) + epsilon) * gain


def norm_back(rows, gain, upstream):
    _, pull = jax.vjp(lambda inner_rows: rms_norm(inner_rows, gain), rows)
    return pull(upstream)[0]


def contract_last(left, right):
    return lax.dot_general(
        left, right, (((1,), (1,)), ((), ())), preferred_element_type=jnp.float32
    )


def contract_first(left, right):
    return lax.dot_general(
        left, right, (((0,), (0,)), ((), ())), preferred_element_type=jnp.float32
    )


def shards(
    tokens, cotangent, norm_gain, up_proj, down_proj, mom_up, mom_down, share_table, module_slot
):
    scale_in = 1.0 / math.sqrt(D)
    scale_out = 1.0 / math.sqrt(FF)
    tok_rows = tokens[0]
    cot_rows = cotangent[0]
    norm_gains = norm_gain[0]
    up_local = up_proj[0]
    down_local = down_proj[0]
    tok_all, cot_all = (
        lax.all_gather(tok_rows, "fsdp", axis=0, tiled=True),
        lax.all_gather(cot_rows, "fsdp", axis=0, tiled=True),
    )
    tok_float = tok_all.astype(jnp.float32)
    first_normed = rms_norm(tok_float, norm_gains[0]).astype(jnp.bfloat16)
    first_pre = jnp.dot(first_normed, up_local[0], preferred_element_type=jnp.float32) * scale_in
    first_hidden = gelu_tanh(first_pre).astype(jnp.bfloat16)
    hidden_summed = lax.psum(
        (contract_last(first_hidden, down_local[0]) * scale_out).astype(jnp.bfloat16), "fsdp"
    ).astype(jnp.float32)
    second_input = tok_float + hidden_summed
    second_normed = rms_norm(second_input, norm_gains[1]).astype(jnp.bfloat16)
    second_pre = jnp.dot(second_normed, up_local[1], preferred_element_type=jnp.float32) * scale_in
    second_hidden = gelu_tanh(second_pre).astype(jnp.bfloat16)
    grad_down_upper = contract_first(cot_all, second_hidden) * scale_out
    second_slope = (
        jnp.dot(cot_all, down_local[1], preferred_element_type=jnp.float32)
        * scale_out
        * gelu_slope(second_pre)
    ).astype(jnp.bfloat16)
    grad_up_upper = contract_first(second_normed, second_slope) * scale_in
    upper_delta = jnp.stack([grad_up_upper, grad_down_upper]).astype(jnp.bfloat16)[None]
    back_summed = lax.psum(
        (contract_last(second_slope, up_local[1]) * scale_in).astype(jnp.bfloat16), "fsdp"
    ).astype(jnp.float32)
    first_grad = (
        cot_all.astype(jnp.float32) + norm_back(second_input, norm_gains[1], back_summed)
    ).astype(jnp.bfloat16)
    grad_down_lower = contract_first(first_grad, first_hidden) * scale_out
    first_slope = (
        jnp.dot(first_grad, down_local[0], preferred_element_type=jnp.float32)
        * scale_out
        * gelu_slope(first_pre)
    ).astype(jnp.bfloat16)
    grad_up_lower = contract_first(first_normed, first_slope) * scale_in
    lower_delta = jnp.stack([grad_up_lower, grad_down_lower]).astype(jnp.bfloat16)[None]
    path_count = share_table.shape[0]
    level_count = share_table.shape[1]
    stacked = jnp.concatenate((lower_delta, upper_delta), axis=0)
    exchanged = lax.all_to_all(stacked, "path", split_axis=2, concat_axis=0, tiled=True)
    received = exchanged.reshape((path_count, level_count) + exchanged.shape[1:])
    module_count = module_slot.shape[0]
    module_ids = jnp.arange(level_count, dtype=jnp.int32)[None, :] * PER_LEVEL + share_table
    id_match = (
        module_ids[:, :, None] == jnp.arange(module_count, dtype=jnp.int32)[None, None, :]
    ).astype(jnp.int32)
    slot_of = jnp.sum(id_match * module_slot[None, None, :], axis=-1).reshape(-1)
    selector = slot_of[None, :] == jnp.arange(module_count, dtype=jnp.int32)[:, None]
    counts = jnp.sum(selector.astype(jnp.float32), axis=1)
    flattened = received.reshape(path_count * level_count, -1)
    summed = jnp.dot(selector.astype(jnp.bfloat16), flattened, preferred_element_type=jnp.float32)
    pseudo = summed / jnp.maximum(counts, 1.0)[:, None]
    row_block = mom_up.shape[1]
    col_block = mom_up.shape[2]
    momentum = jnp.stack((mom_up, mom_down), axis=1).reshape(module_count, -1)
    new_momentum = momentum_decay * momentum + pseudo
    outer_step = (pseudo + momentum_decay * new_momentum).astype(jnp.bfloat16)
    routed = jnp.dot(
        selector.T.astype(jnp.bfloat16), outer_step, preferred_element_type=jnp.float32
    ).astype(jnp.bfloat16)
    routed = routed.reshape(path_count, level_count, 2, row_block, col_block)
    returned = lax.all_to_all(routed, "path", split_axis=0, concat_axis=3, tiled=True)
    new_up = (
        up_proj.astype(jnp.float32) - outer_rate * returned[:, :, 0].astype(jnp.float32)
    ).astype(jnp.bfloat16)
    new_down = (
        down_proj.astype(jnp.float32) - outer_rate * returned[:, :, 1].astype(jnp.float32)
    ).astype(jnp.bfloat16)
    new_momentum = new_momentum.reshape(module_count, 2, row_block, col_block)
    return (new_up, new_down, new_momentum[:, 0], new_momentum[:, 1])


def solution(mesh):
    in_specs = (
        P("path", "fsdp", None),
        P("path", "fsdp", None),
        P("path", None, None),
        P("path", None, None, "fsdp"),
        P("path", None, None, "fsdp"),
        P(None, "path", "fsdp"),
        P(None, "path", "fsdp"),
        P(),
        P(),
    )
    out_specs = (
        P("path", None, None, "fsdp"),
        P("path", None, None, "fsdp"),
        P(None, "path", "fsdp"),
        P(None, "path", "fsdp"),
    )
    return jax.shard_map(shards, mesh=mesh, in_specs=in_specs, out_specs=out_specs, check_vma=False)
```

profile of v0, /device:TPU:84, one launch (start us, length us, event | category | flops | bytes accessed | tf_op | source)
XLA Modules:
  0.0 688.4 jit_solution(12021186068718055851)
XLA Ops:
  8.8 33.1 %all-gather.5.cloned.1.call-done = bf16[1,1024,2048]{2,1,0:T(8,128)(2,1)} async-done(((bf16[1,128,2048]{2,1,0:T(8,128)(2,1)}), bf16[1,1024,2048]{2,1,0:T(8,128)(2,1)}) %all-gather.5.cloned.1.call-update) | async-done | bytes 4194320 | tf_op jit(solution)/shard_map/all_gather | solution.py:65
  50.8 4.6 multiply_convert_fusion.2
  56.4 68.4 %all-reduce.3.cloned.1.call-done = bf16[1024,2048]{1,0:T(8,128)(2,1)} async-done(((bf16[1024,2048]{1,0:T(8,128)(2,1)}), bf16[1024,2048]{1,0:T(8,128)(2,1)}) %all-reduce.3.cloned.1.call-update) | async-done | bytes 4194320 | tf_op jit(solution)/shard_map/psum | solution.py:72
  124.8 5.0 multiply_reduce_fusion.1
  134.8 26.9 %all-gather.7.cloned.1.call-done = bf16[1,1024,2048]{2,1,0:T(8,128)(2,1)} async-done(((bf16[1,128,2048]{2,1,0:T(8,128)(2,1)}), bf16[1,1024,2048]{2,1,0:T(8,128)(2,1)}) %all-gather.7.cloned.1.call-update) | async-done | bytes 4194320 | tf_op jit(solution)/shard_map/all_gather | solution.py:66
  161.8 6.4 multiply_convert_fusion.9
  172.7 5.5 fusion.16
  178.2 5.0 fusion.15
  183.2 58.9 %all-reduce.5.cloned.1.call-done = bf16[1024,2048]{1,0:T(8,128)(2,1)} async-done(((bf16[1024,2048]{1,0:T(8,128)(2,1)}), bf16[1024,2048]{1,0:T(8,128)(2,1)}) %all-reduce.5.cloned.1.call-update) | async-done | bytes 4194320 | tf_op jit(solution)/shard_map/psum | solution.py:87
  242.1 6.8 multiply_reduce_fusion
  250.4 6.9 %fusion.1 = bf16[1024,2048]{1,0:T(8,128)(2,1)S(1)} fusion(bf16[1024,2048]{1,0:T(8,128)(2,1)S(1)} %copy-done.8, bf16[1024,2048]{1,0:T(8,128)(2,1)S(1)} %copy-done.7, bf16[1,1024,2048]{2,1,0:T(8,128)(2,1)} %all-gather.7.cloned.1.call-done, bf16[1,1024,2048]{2,1,0:T(8,128)(2,1)S(1)} %copy-done.3, f32[1024]{0:T(1024)S(1)} %multiply_multiply_fusion, ...), kind=kLoop, calls=%fused_computation.7 | loop fusion | flops 25165824 | bytes 20987904 | tf_op jit(solution)/shard_map/convert_element_type | solution.py:92
  263.3 11.9 %fusion.13 = bf16[1,1,2048,512]{3,2,1,0:T(8,128)(2,1)} fusion(bf16[1,1024,2048]{2,1,0:T(8,128)(2,1)} %all-gather.5.cloned.1.call-done, f32[2048]{0:T(1024)S(1)} %bitcast.112, f32[1024]{0:T(1024)S(1)} %add_rsqrt_fusion, f32[1024,512]{1,0:T(8,128)} %copy-done.17, bf16[1024,2048]{1,0:T(8,128)(2,1)} %copy-done.12, bf16[1,2,2048,512]{3,2,1,0:T(8,128)(2,1)} %param.13), kind=kOutput, calls=%fused_computation.35 | convolution fusion | flops 4316463104 | bytes 14692352 | tf_op jit(solution)/shard_map/dot_general | solution.py:49
  278.9 29.4 %copy.36 = bf16[2,2,2048,512]{3,1,0,2:T(2,128)(2,1)} copy(bf16[2,2,2048,512]{3,2,1,0:T(8,128)(2,1)S(1)} %maximum_maximum_fusion) | data formatting | bytes 16777216 | tf_op jit(solution)/shard_map/concatenate | solution.py:103
  308.3 7.4 %all-to-all-start = ((bf16[2,2,2048,512]{3,1,0,2:T(2,128)(2,1)}), bf16[2,2,2048,512]{3,1,0,2:T(2,128)(2,1)}, u32[]{:S(2)}, u32[]{:S(2)}) async-start(bf16[2,2,2048,512]{3,1,0,2:T(2,128)(2,1)} %copy.36), calls=%async_computation | async-start | bytes 16777216 | tf_op jit(solution)/shard_map/all_to_all | solution.py:104
  322.9 145.2 %all-to-all-done = bf16[2,2,2048,512]{3,1,0,2:T(2,128)(2,1)} async-done(((bf16[2,2,2048,512]{3,1,0,2:T(2,128)(2,1)}), bf16[2,2,2048,512]{3,1,0,2:T(2,128)(2,1)}, u32[]{:S(2)}, u32[]{:S(2)}) %all-to-all-start) | async-done | bytes 8388640 | tf_op jit(solution)/shard_map/all_to_all | solution.py:104
  468.1 9.0 %copy.49 = bf16[2,2,16,128,512]{4,3,1,0,2:T(8,128)(2,1)} copy(bf16[2,2,16,128,512]{4,1,0,3,2:T(2,128)(2,1)} %bitcast.14) | data formatting | bytes 16777216 | tf_op jit(solution)/shard_map/all_to_all | solution.py:104
  477.2 8.9 %reshape_reshape.3 = bf16[32,131072]{1,0:T(8,128)(2,1)} reshape(bf16[16,2,2,128,512]{4,3,2,1,0:T(8,128)(2,1)} %bitcast.103) | data formatting | bytes 16777216 | tf_op jit(solution)/shard_map/reshape;reshape | solution.py:114
  486.1 5.8 fusion.65
  491.9 4.9 convolution_convert_fusion
  496.8 9.8 %copy.45 = bf16[4,8,256,512]{3,2,1,0:T(8,128)(2,1)} copy(bf16[4,8,256,512]{3,1,2,0:T(8,128)(2,1)} %bitcast.101) | data formatting | bytes 16777216
  506.7 7.2 %all-to-all-start.1 = ((bf16[16,2,2,128,512]{4,3,2,1,0:T(8,128)(2,1)}), bf16[16,2,2,128,512]{4,3,2,1,0:T(8,128)(2,1)}, u32[]{:S(2)}, u32[]{:S(2)}) async-start(bf16[16,2,2,128,512]{4,3,2,1,0:T(8,128)(2,1)} %bitcast.102), calls=%async_computation.1 | async-start | bytes 16777216 | tf_op jit(solution)/shard_map/all_to_all | solution.py:126
  521.0 144.9 %all-to-all-done.1 = bf16[16,2,2,128,512]{4,3,2,1,0:T(8,128)(2,1)} async-done(((bf16[16,2,2,128,512]{4,3,2,1,0:T(8,128)(2,1)}), bf16[16,2,2,128,512]{4,3,2,1,0:T(8,128)(2,1)}, u32[]{:S(2)}, u32[]{:S(2)}) %all-to-all-start.1) | async-done | bytes 8388640 | tf_op jit(solution)/shard_map/all_to_all | solution.py:126
  665.9 7.8 %copy.39 = bf16[1,2,2,16,128,512]{5,4,3,1,2,0:T(8,128)(2,1)} copy(bf16[1,2,2,16,128,512]{5,4,2,1,3,0:T(8,128)(2,1)} %bitcast.20) | data formatting | bytes 16777216 | tf_op jit(solution)/shard_map/all_to_all | solution.py:126
  673.7 8.0 %fusion.5 = (bf16[1,2,2048,512]{3,2,1,0:T(8,128)(2,1)}, bf16[1,2,2048,512]{3,2,1,0:T(8,128)(2,1)}) fusion(bf16[1,2,2048,512]{3,2,1,0:T(8,128)(2,1)S(1)} %copy-done.10, bf16[1,2,2,2048,512]{4,3,1,2,0:T(8,128)(2,1)} %bitcast.100, bf16[1,2,2048,512]{3,2,1,0:T(8,128)(2,1)} %param.12), kind=kLoop, calls=%fused_computation.13 | loop fusion | flops 20971520 | bytes 25165824 | tf_op jit(solution)/shard_map/convert_element_type | solution.py:132
  (67 shorter events, 46.4 us)
Async XLA Ops:
  7.2 34.7 %all-gather.5.cloned.1.call-start = ((), (), s32[]{:S(2)}) async-start(), calls=%async_computation.4 | async-start | bytes 4718592 | tf_op jit(solution)/shard_map/all_gather | solution.py:65
  7.9 116.9 %all-reduce.3.cloned.1.call-start = ((), (), s32[]{:S(2)}) async-start(), calls=%async_computation.2 | async-start | bytes 8388608 | tf_op jit(solution)/shard_map/psum | solution.py:72
  41.9 3.4 copy-start
  45.3 5.5 copy-start.9
  55.5 106.3 %all-gather.7.cloned.1.call-start = ((), (), s32[]{:S(2)}) async-start(), calls=%async_computation.5 | async-start | bytes 4718592 | tf_op jit(solution)/shard_map/all_gather | solution.py:66
  56.2 185.9 %all-reduce.5.cloned.1.call-start = ((), (), s32[]{:S(2)}) async-start(), calls=%async_computation.3 | async-start | bytes 8388608 | tf_op jit(solution)/shard_map/psum | solution.py:87
  124.8 5.0 copy-start.1
  124.8 5.9 copy-start.5
  134.8 33.4 %copy-start.16 = (f32[1024,512]{1,0:T(8,128)}, f32[1024,512]{1,0:T(8,128)S(1)}, u32[]{:S(2)}) copy-start(f32[1024,512]{1,0:T(8,128)S(1)} %fusion.24) | copy-start | bytes 6291460
  161.8 6.5 copy-start.11
  172.7 5.6 copy-start.2
  172.7 5.6 copy-start.6
  242.1 6.8 copy-start.3
  242.1 7.1 %copy-start.7 = (bf16[1024,2048]{1,0:T(8,128)(2,1)S(1)}, bf16[1024,2048]{1,0:T(8,128)(2,1)}, u32[]{:S(2)}) copy-start(bf16[1024,2048]{1,0:T(8,128)(2,1)} %all-reduce.3.cloned.1.call-done) | copy-start | bytes 12582916
  242.1 8.3 %copy-start.8 = (bf16[1024,2048]{1,0:T(8,128)(2,1)S(1)}, bf16[1024,2048]{1,0:T(8,128)(2,1)}, u32[]{:S(2)}) copy-start(bf16[1024,2048]{1,0:T(8,128)(2,1)} %all-reduce.5.cloned.1.call-done) | copy-start | bytes 12582916
  250.4 8.9 %copy-start.18 = (f32[1024,512]{1,0:T(8,128)S(1)}, f32[1024,512]{1,0:T(8,128)}, u32[]{:S(2)}) copy-start(f32[1024,512]{1,0:T(8,128)} %copy-done.17) | copy-start | bytes 6291460
  257.3 2.0 copy-start.12
  308.3 7.4 %copy-start.14 = (s32[16,2]{0,1:T(2,128)S(1)}, s32[16,2]{0,1:T(2,128)}, u32[]{:S(2)}) copy-start(s32[16,2]{0,1:T(2,128)} %param.16) | copy-start | bytes 388
  308.3 7.5 %copy-start.15 = (s32[8]{0:T(128)S(1)}, s32[8]{0:T(128)}, u32[]{:S(2)}) copy-start(s32[8]{0:T(128)} %param.17) | copy-start | bytes 100
  308.3 7.7 %copy-start.13 = (f32[8,128,512]{2,1,0:T(8,128)S(1)}, f32[8,128,512]{2,1,0:T(8,128)}, u32[]{:S(2)}) copy-start(f32[8,128,512]{2,1,0:T(8,128)} %param.15) | copy-start | bytes 6291460
  308.3 159.9 %all-to-all-start = ((bf16[2,2,2048,512]{3,1,0,2:T(2,128)(2,1)}), bf16[2,2,2048,512]{3,1,0,2:T(2,128)(2,1)}, u32[]{:S(2)}, u32[]{:S(2)}) async-start(bf16[2,2,2048,512]{3,1,0,2:T(2,128)(2,1)} %copy.36), calls=%async_computation | async-start | bytes 16777216 | tf_op jit(solution)/shard_map/all_to_all | solution.py:104
  491.9 4.9 copy-start.4
  506.7 159.3 %all-to-all-start.1 = ((bf16[16,2,2,128,512]{4,3,2,1,0:T(8,128)(2,1)}), bf16[16,2,2,128,512]{4,3,2,1,0:T(8,128)(2,1)}, u32[]{:S(2)}, u32[]{:S(2)}) async-start(bf16[16,2,2,128,512]{4,3,2,1,0:T(8,128)(2,1)} %bitcast.102), calls=%async_computation.1 | async-start | bytes 16777216 | tf_op jit(solution)/shard_map/all_to_all | solution.py:126
  665.9 7.8 %copy-start.10 = (bf16[1,2,2048,512]{3,2,1,0:T(8,128)(2,1)S(1)}, bf16[1,2,2048,512]{3,2,1,0:T(8,128)(2,1)}, u32[]{:S(2)}) copy-start(bf16[1,2,2048,512]{3,2,1,0:T(8,128)(2,1)} %param.13) | copy-start | bytes 12582916
  (1 other events, 1.3 us)
Sparse Core Ops, SparseCore 0:
  9.7 32.1 all-gather.4
  55.6 69.1 all-reduce.2
  126.5 35.1 all-gather.6
  172.8 69.2 all-reduce.4
where the time goes:
time: 693 us; the launch traced here: 688 us
  waiting for transfers between devices  479 us (69%)
  local copies, waits for them, and re-layouts  83.5 us (12%)
  matrix products  60.7 us (9%)
  other arithmetic  36.2 us (5%)
  starting transfers between devices  14.9 us (2%)
  between operations  14.2 us (2%)
    all_to_all x1, waiting for transfers between devices, shards(): lax.all_to_all(stacked, 'path', split_axis=2, concat_axis=0, tiled=True)  145 us
    all_to_all x1, waiting for transfers between devices, shards(): lax.all_to_all(routed, 'path', split_axis=0, concat_axis=3, tiled=True)  145 us
    psum x1, waiting for transfers between devices, shards(): lax.psum((contract_last(first_hidden, down_local[0]) * scale_out).astype(...  68.4 us
    psum x1, waiting for transfers between devices, shards(): lax.psum((contract_last(second_slope, up_local[1]) * scale_in).astype(jnp...  58.9 us
    all_gather x1, waiting for transfers between devices, shards(): lax.all_gather(tok_rows, 'fsdp', axis=0, tiled=True)  33.1 us
    concatenate x1, local copies, waits for them, and re-layouts, shards(): stacked = jnp.concatenate((lower_delta, upper_delta), axis=0)  29.4 us
    all_gather x1, waiting for transfers between devices, shards(): lax.all_gather(cot_rows, 'fsdp', axis=0, tiled=True)  26.9 us
    dot_general x4, matrix products, contract_first(): lax.dot_general(left, right, (((0,), (0,)), ((), ())), preferred_element_...  26.3 us
  transfers between devices with their start and end apart: 6, of which 6 were waited for; matrix products, arithmetic and copies ran while one was open for 5% of the time, Pallas kernels for 0%

commit v1 on v0

v1 whole, which is shorter than its diff:
```python
import functools
import math

import jax
import jax.numpy as jnp
from jax import lax
from jax.experimental import pallas as pl
from jax.experimental.pallas import tpu as pltpu
from jax.sharding import PartitionSpec as P

PER_LEVEL = 4

epsilon = 1e-06
gelu_coef = 0.7978845608
cubic_coef = 0.044715
momentum_decay = 0.9
outer_rate = 0.7


def gelu_tanh(value):
    inner = gelu_coef * (value + cubic_coef * value * value * value)
    return 0.5 * value * (1.0 + jnp.tanh(inner))


def gelu_slope(value):
    inner = gelu_coef * (value + cubic_coef * value * value * value)
    tangent = jnp.tanh(inner)
    return 0.5 * (1.0 + tangent) + 0.5 * value * (1.0 - tangent * tangent) * gelu_coef * (
        1.0 + 3.0 * cubic_coef * value * value
    )


def rms_norm(rows, gain):
    return rows * lax.rsqrt(jnp.mean(rows * rows, axis=-1, keepdims=True) + epsilon) * gain


def norm_back(rows, gain, upstream):
    _, pull = jax.vjp(lambda inner_rows: rms_norm(inner_rows, gain), rows)
    return pull(upstream)[0]


def contract_last(left, right):
    return lax.dot_general(
        left, right, (((1,), (1,)), ((), ())), preferred_element_type=jnp.float32
    )


def contract_first(left, right):
    return lax.dot_general(
        left, right, (((0,), (0,)), ((), ())), preferred_element_type=jnp.float32
    )


def combine_body(level, paths, share_ref, slot_ref, *refs):
    recv_up, recv_down, mom_up, mom_down = refs[:4]
    out_up, out_down, send_up, send_down, acc_up, acc_down = refs[-6:]
    module = pl.program_id(1)
    acc_up[...] = jnp.zeros_like(acc_up)
    acc_down[...] = jnp.zeros_like(acc_down)
    count = jnp.float32(0.0)
    for path in range(paths):
        hit = share_ref[path, level] == module
        count = count + jnp.where(hit, 1.0, 0.0)

        @pl.when(hit)
        def _():
            acc_up[...] += recv_up[path].astype(jnp.float32)
            acc_down[...] += recv_down[path].astype(jnp.float32)

    inverse = 1.0 / jnp.full((1, acc_up.shape[1]), jnp.maximum(count, 1.0), jnp.float32)
    for acc, mom, out in ((acc_up, mom_up, out_up), (acc_down, mom_down, out_down)):
        pseudo = acc[...] * inverse
        fresh = momentum_decay * mom[0] + pseudo
        out[0] = fresh
        acc[...] = pseudo + momentum_decay * fresh
    for path in range(paths):

        @pl.when(share_ref[path, level] == module)
        def _():
            send_up[path] = acc_up[...].astype(jnp.bfloat16)
            send_down[path] = acc_down[...].astype(jnp.bfloat16)


def combine(level, share, slots, recv_up, recv_down, mom_up, mom_down, partial):
    paths, rows, cols = recv_up.shape
    step = 32
    mom_spec = pl.BlockSpec(
        (1, step, cols), lambda r, m, share, slots: (slots[level * PER_LEVEL + m], r, 0)
    )
    path_spec = pl.BlockSpec((paths, step, cols), lambda r, m, share, slots: (0, r, 0))
    hold = [pl.BlockSpec(memory_space=pl.ANY)] * len(partial)
    return pl.pallas_call(
        functools.partial(combine_body, level, paths),
        grid_spec=pltpu.PrefetchScalarGridSpec(
            num_scalar_prefetch=2,
            grid=(rows // step, PER_LEVEL),
            in_specs=[path_spec, path_spec, mom_spec, mom_spec] + hold,
            out_specs=[mom_spec, mom_spec, path_spec, path_spec],
            scratch_shapes=[pltpu.VMEM((step, cols), jnp.float32)] * 2,
        ),
        out_shape=[
            jax.ShapeDtypeStruct(mom_up.shape, jnp.float32),
            jax.ShapeDtypeStruct(mom_up.shape, jnp.float32),
            jax.ShapeDtypeStruct(recv_up.shape, jnp.bfloat16),
            jax.ShapeDtypeStruct(recv_up.shape, jnp.bfloat16),
        ],
        input_output_aliases={6: 0, 7: 1} if partial else {},
        cost_estimate=pl.CostEstimate(
            flops=8 * recv_up.size, bytes_accessed=16 * recv_up.size, transcendentals=0
        ),
        name="combine",
    )(share, slots, recv_up, recv_down, mom_up, mom_down, *partial)


def update_body(up_ref, down_ref, back_up, back_down, *refs):
    new_up, new_down = refs[-2:]
    for old, back, new in ((up_ref, back_up, new_up), (down_ref, back_down, new_down)):
        new[0, 0] = (
            old[0, 0].astype(jnp.float32) - outer_rate * back[...].astype(jnp.float32)
        ).astype(jnp.bfloat16)


def update(level, up, down, back_up, back_down, partial):
    _, _, rows, cols = up.shape
    step = 512
    full = pl.BlockSpec((1, 1, step, cols), lambda r: (0, level, r, 0))
    flat = pl.BlockSpec((step, cols), lambda r: (r, 0))
    hold = [pl.BlockSpec(memory_space=pl.ANY)] * len(partial)
    return pl.pallas_call(
        update_body,
        grid=(rows // step,),
        in_specs=[full, full, flat, flat] + hold,
        out_specs=[full, full],
        out_shape=[jax.ShapeDtypeStruct(up.shape, up.dtype)] * 2,
        input_output_aliases={4: 0, 5: 1} if partial else {},
        cost_estimate=pl.CostEstimate(
            flops=4 * rows * cols, bytes_accessed=12 * rows * cols, transcendentals=0
        ),
        name="update",
    )(up, down, back_up.reshape(rows, cols), back_down.reshape(rows, cols), *partial)


def swap(value):
    return lax.all_to_all(value, "path", split_axis=0, concat_axis=0, tiled=True)


def shards(
    tokens, cotangent, norm_gain, up_proj, down_proj, mom_up, mom_down, share_table, module_slot
):
    scale_in = 1.0 / math.sqrt(2048)
    scale_out = 1.0 / math.sqrt(4096)
    norm_gains = norm_gain[0]
    up_local = up_proj[0]
    down_local = down_proj[0]
    paths = share_table.shape[0]
    row_block, col_block = mom_up.shape[1:]

    def blocks(grad):
        return grad.astype(jnp.bfloat16).reshape(paths, row_block, col_block)

    def exchange(level, grad_up, grad_down, partial):
        recv_up, recv_down = swap(blocks(grad_up)), swap(blocks(grad_down))
        return combine(
            level, share_table, module_slot, recv_up, recv_down, mom_up, mom_down, partial
        )

    tok_all, cot_all = (
        lax.all_gather(tokens[0], "fsdp", axis=0, tiled=True),
        lax.all_gather(cotangent[0], "fsdp", axis=0, tiled=True),
    )
    tok_float = tok_all.astype(jnp.float32)
    first_normed = rms_norm(tok_float, norm_gains[0]).astype(jnp.bfloat16)
    first_pre = jnp.dot(first_normed, up_local[0], preferred_element_type=jnp.float32) * scale_in
    first_hidden = gelu_tanh(first_pre).astype(jnp.bfloat16)
    hidden_summed = lax.psum(
        (contract_last(first_hidden, down_local[0]) * scale_out).astype(jnp.bfloat16), "fsdp"
    ).astype(jnp.float32)
    second_input = tok_float + hidden_summed
    second_normed = rms_norm(second_input, norm_gains[1]).astype(jnp.bfloat16)
    second_pre = jnp.dot(second_normed, up_local[1], preferred_element_type=jnp.float32) * scale_in
    second_hidden = gelu_tanh(second_pre).astype(jnp.bfloat16)
    grad_down_upper = contract_first(cot_all, second_hidden) * scale_out
    second_slope = (
        jnp.dot(cot_all, down_local[1], preferred_element_type=jnp.float32)
        * scale_out
        * gelu_slope(second_pre)
    ).astype(jnp.bfloat16)
    grad_up_upper = contract_first(second_normed, second_slope) * scale_in
    mom_up_1, mom_down_1, send_up_1, send_down_1 = exchange(1, grad_up_upper, grad_down_upper, ())
    back_summed = lax.psum(
        (contract_last(second_slope, up_local[1]) * scale_in).astype(jnp.bfloat16), "fsdp"
    ).astype(jnp.float32)
    first_grad = (
        cot_all.astype(jnp.float32) + norm_back(second_input, norm_gains[1], back_summed)
    ).astype(jnp.bfloat16)
    grad_down_lower = contract_first(first_grad, first_hidden) * scale_out
    first_slope = (
        jnp.dot(first_grad, down_local[0], preferred_element_type=jnp.float32)
        * scale_out
        * gelu_slope(first_pre)
    ).astype(jnp.bfloat16)
    grad_up_lower = contract_first(first_normed, first_slope) * scale_in
    new_mom_up, new_mom_down, send_up_0, send_down_0 = exchange(
        0, grad_up_lower, grad_down_lower, (mom_up_1, mom_down_1)
    )
    partial = update(1, up_proj, down_proj, swap(send_up_1), swap(send_down_1), ())
    new_up, new_down = update(0, up_proj, down_proj, swap(send_up_0), swap(send_down_0), partial)
    return (new_up, new_down, new_mom_up, new_mom_down)


def solution(mesh):
    in_specs = (
        P("path", "fsdp", None),
        P("path", "fsdp", None),
        P("path", None, None),
        P("path", None, None, "fsdp"),
        P("path", None, None, "fsdp"),
        P(None, "path", "fsdp"),
        P(None, "path", "fsdp"),
        P(),
        P(),
    )
    out_specs = (
        P("path", None, None, "fsdp"),
        P("path", None, None, "fsdp"),
        P(None, "path", "fsdp"),
        P(None, "path", "fsdp"),
    )
    return jax.shard_map(shards, mesh=mesh, in_specs=in_specs, out_specs=out_specs, check_vma=False)
```

time: 693 us -> 464 us (0.67)
  the two profiles are of different devices: /device:TPU:84 before, /device:TPU:0 now
where the time goes in v1:
time: 464 us; the launch traced here: 458 us
  waiting for transfers between devices  232 us (50%)
  blocking collectives  58.6 us (13%)
  matrix products  49.6 us (11%)
  Pallas kernels  39.5 us (9%)
  starting transfers between devices  28.4 us (6%)
  other arithmetic  21.9 us (5%)
  between operations  14.2 us (3%)
  local copies, waits for them, and re-layouts  13.5 us (3%)
    all_to_all x6, waiting for transfers between devices, swap(): lax.all_to_all(value, 'path', split_axis=0, concat_axis=0, tiled=True)  99.6 us
    psum x1, waiting for transfers between devices, shards(): lax.psum((contract_last(first_hidden, down_local[0]) * scale_out).astype(...  71.7 us
    all_to_all x2, blocking collectives, swap(): lax.all_to_all(value, 'path', split_axis=0, concat_axis=0, tiled=True)  58.6 us
    all_gather x1, waiting for transfers between devices, shards(): lax.all_gather(tokens[0], 'fsdp', axis=0, tiled=True)  35.5 us
    pallas_call x2, Pallas kernels, combine(): pl.pallas_call(functools.partial(combine_body, level, paths), grid_spec=p...  28 us
    all_to_all x6, starting transfers between devices, swap(): lax.all_to_all(value, 'path', split_axis=0, concat_axis=0, tiled=True)  27.5 us
    all_gather x1, waiting for transfers between devices, shards(): lax.all_gather(cotangent[0], 'fsdp', axis=0, tiled=True)  23.9 us
    dot_general x4, matrix products, contract_first(): lax.dot_general(left, right, (((0,), (0,)), ((), ())), preferred_element_...  20.8 us
  transfers between devices with their start and end apart: 10, of which 9 were waited for; matrix products, arithmetic and copies ran while one was open for 12% of the time, Pallas kernels for 7%

profile of v1, /device:TPU:0, one launch (start us, length us, event | category | flops | bytes accessed | tf_op | source)
XLA Modules:
  0.0 457.5 jit_solution(3602921773203756114)
XLA Ops:
  8.8 35.5 %all-gather.5.cloned.1.call-done = bf16[1,1024,2048]{2,1,0:T(8,128)(2,1)} async-done(((bf16[1,128,2048]{2,1,0:T(8,128)(2,1)}), bf16[1,1024,2048]{2,1,0:T(8,128)(2,1)}) %all-gather.5.cloned.1.call-update) | async-done | bytes 4194320 | tf_op jit(solution)/shard_map/all_gather | solution.py:168
  53.2 4.6 %multiply_convert_fusion.2 = bf16[1024,2048]{1,0:T(8,128)(2,1)} fusion(bf16[1,2,2048,512]{3,2,1,0:T(8,128)(2,1)S(1)} %copy-done.7, f32[1024,512]{1,0:T(8,128)S(1)} %fusion.24), kind=kOutput, calls=%fused_computation.14 | convolution fusion | flops 2156920832 | bytes 8388608 | tf_op jit(solution)/shard_map/dot_general | solution.py:43
  58.6 71.7 %all-reduce.3.cloned.1.call-done = bf16[1024,2048]{1,0:T(8,128)(2,1)} async-done(((bf16[1024,2048]{1,0:T(8,128)(2,1)}), bf16[1024,2048]{1,0:T(8,128)(2,1)}) %all-reduce.3.cloned.1.call-update) | async-done | bytes 4194320 | tf_op jit(solution)/shard_map/psum | solution.py:175
  130.3 5.0 %multiply_reduce_fusion.1 = f32[1024]{0:T(1024)S(1)} fusion(bf16[1024,2048]{1,0:T(8,128)(2,1)} %all-reduce.3.cloned.1.call-done, bf16[1,1024,2048]{2,1,0:T(8,128)(2,1)} %all-gather.5.cloned.1.call-done), kind=kLoop, calls=%fused_computation.13 | loop fusion | flops 10484736 | bytes 8392704 | tf_op jit(solution)/shard_map/reduce_sum | solution.py:34
  140.3 23.9 %all-gather.7.cloned.1.call-done = bf16[1,1024,2048]{2,1,0:T(8,128)(2,1)} async-done(((bf16[1,128,2048]{2,1,0:T(8,128)(2,1)}), bf16[1,1024,2048]{2,1,0:T(8,128)(2,1)}) %all-gather.7.cloned.1.call-update) | async-done | bytes 4194320 | tf_op jit(solution)/shard_map/all_gather | solution.py:169
  164.2 6.4 %multiply_convert_fusion.9 = bf16[1024,512]{1,0:T(8,128)(2,1)S(1)} fusion(f32[1024,512]{1,0:T(8,128)S(1)} %fusion.19, bf16[1,2,2048,512]{3,2,1,0:T(8,128)(2,1)} %down_ref.3, bf16[1,1024,2048]{2,1,0:T(8,128)(2,1)} %all-gather.7.cloned.1.call-done), kind=kOutput, calls=%fused_computation.41 | convolution fusion | flops 2158493696 | bytes 9437184 | tf_op jit(solution)/shard_map/dot_general | solution.py:184
  175.3 6.9 %all-to-all-start.2 = ((bf16[16,128,512]{2,1,0:T(8,128)(2,1)}), bf16[16,128,512]{2,1,0:T(8,128)(2,1)S(1)}, u32[]{:S(2)}, u32[]{:S(2)}) async-start(bf16[16,128,512]{2,1,0:T(8,128)(2,1)} %bitcast.66), calls=%async_computation.2 | async-start | bytes 4194304 | tf_op jit(solution)/shard_map/all_to_all | solution.py:144
  182.7 6.0 %multiply_convert_fusion = bf16[1024,2048]{1,0:T(8,128)(2,1)} fusion(bf16[1024,512]{1,0:T(8,128)(2,1)S(1)} %multiply_convert_fusion.9, bf16[1,2,2048,512]{3,2,1,0:T(8,128)(2,1)} %up_ref.3), kind=kOutput, calls=%fused_computation.11 | convolution fusion | flops 2151677952 | bytes 7340032 | tf_op jit(solution)/shard_map/dot_general | solution.py:43
  188.8 6.8 %fusion.11 = bf16[2048,512]{0,1:T(8,128)(2,1)} fusion(bf16[1,1024,2048]{2,1,0:T(8,128)(2,1)} %all-gather.7.cloned.1.call-done, f32[1024,512]{1,0:T(8,128)} %copy-done.16), kind=kOutput, calls=%fused_computation.25 | convolution fusion | flops 2154823680 | bytes 8388608 | tf_op jit(solution)/shard_map/dot_general | solution.py:49
  199.5 13.7 %all-to-all-done.2.refs_0_ = bf16[16,128,512]{2,1,0:T(8,128)(2,1)S(1)} async-done(((bf16[16,128,512]{2,1,0:T(8,128)(2,1)}), bf16[16,128,512]{2,1,0:T(8,128)(2,1)S(1)}, u32[]{:S(2)}, u32[]{:S(2)}) %all-to-all-start.2) | async-done | bytes 2097184 | tf_op jit(solution)/shard_map/all_to_all | solution.py:144
  219.8 28.3 %all-to-all-done.3.refs_1_ = bf16[16,128,512]{2,1,0:T(8,128)(2,1)} async-done(((bf16[16,128,512]{2,1,0:T(8,128)(2,1)}), bf16[16,128,512]{2,1,0:T(8,128)(2,1)}, u32[]{:S(2)}, u32[]{:S(2)}) %all-to-all-start.3) | async-done | bytes 2097184 | tf_op jit(solution)/shard_map/all_to_all | solution.py:144
  248.1 14.0 %combine.2 = (f32[8,128,512]{2,1,0:T(8,128)}, f32[8,128,512]{2,1,0:T(8,128)}, bf16[16,128,512]{2,1,0:T(8,128)(2,1)}, bf16[16,128,512]{2,1,0:T(8,128)(2,1)}) custom-call(s32[16,2]{1,0:T(8,128)} %copy.19.share_ref, s32[8]{0:T(128)} %slot_ref.3, bf16[16,128,512]{2,1,0:T(8,128)(2,1)} %copy-done.10, bf16[16,128,512]{2,1,0:T(8,128)(2,1)} %all-to-all-done.3.refs_1_, ...), custom_call_target="tpu_custom_call" | custom-call | flops 8388608 | bytes 16777216 | tf_op jit(solution)/shard_map/combine/pallas_call | solution.py:92
  266.0 6.8 %multiply_reduce_fusion = f32[1024]{0:T(1024)S(1)} fusion(bf16[1024,2048]{1,0:T(8,128)(2,1)} %all-reduce.5.cloned.1.call-done, bf16[1024,2048]{1,0:T(8,128)(2,1)} %all-reduce.3.cloned.1.call-done, bf16[1,1024,2048]{2,1,0:T(8,128)(2,1)} %all-gather.5.cloned.1.call-done, f32[2048]{0:T(1024)S(1)} %bitcast.71), kind=kLoop, calls=%fused_computation.9 | loop fusion | flops 14679040 | bytes 12595200 | tf_op jit(solution)/shard_map/transpose(jvp())/reduce_sum | solution.py:34
  274.3 6.9 %fusion.1 = bf16[1024,2048]{1,0:T(8,128)(2,1)S(1)} fusion(bf16[1024,2048]{1,0:T(8,128)(2,1)S(1)} %copy-done.9, bf16[1024,2048]{1,0:T(8,128)(2,1)S(1)} %copy-done.6, bf16[1,1024,2048]{2,1,0:T(8,128)(2,1)} %all-gather.7.cloned.1.call-done, bf16[1,1024,2048]{2,1,0:T(8,128)(2,1)S(1)} %copy-done.3, f32[1024]{0:T(1024)S(1)} %multiply_multiply_fusion, ...), kind=kLoop, calls=%fused_computation.5 | loop fusion | flops 25165824 | bytes 20987904 | tf_op jit(solution)/shard_map/convert_element_type | solution.py:195
  288.8 4.8 %all-to-all-done.6 = bf16[16,128,512]{2,1,0:T(8,128)(2,1)S(1)} async-done(((bf16[16,128,512]{2,1,0:T(8,128)(2,1)}), bf16[16,128,512]{2,1,0:T(8,128)(2,1)S(1)}, u32[]{:S(2)}, u32[]{:S(2)}) %all-to-all-start.6) | async-done | bytes 2097184 | tf_op jit(solution)/shard_map/all_to_all | solution.py:144
  299.6 5.4 %multiply_convert_fusion.5 = bf16[2048,512]{1,0:T(8,128)(2,1)S(1)} fusion(bf16[1024,2048]{1,0:T(8,128)(2,1)} %copy-done.14, f32[1024,512]{1,0:T(8,128)} %copy-done.17), kind=kOutput, calls=%fused_computation.21 | convolution fusion | flops 2154823680 | bytes 8388608 | tf_op jit(solution)/shard_map/dot_general | solution.py:49
  305.0 22.3 %all-to-all-done.refs_0_ = bf16[16,128,512]{2,1,0:T(8,128)(2,1)} async-done(((bf16[16,128,512]{2,1,0:T(8,128)(2,1)}), bf16[16,128,512]{2,1,0:T(8,128)(2,1)}, u32[]{:S(2)}, u32[]{:S(2)}) %all-to-all-start) | async-done | bytes 2097184 | tf_op jit(solution)/shard_map/all_to_all | solution.py:144
  327.3 30.4 %all_to_all.40.refs_1_ = bf16[16,128,512]{2,1,0:T(8,128)(2,1)} all-to-all(bf16[16,128,512]{2,1,0:T(8,128)(2,1)S(1)} %bitcast.68), channel_id=1, replica_groups=mesh['path'=16,'fsdp'=8] {'path'}, dimensions={0} | all-to-all | bytes 4194304 | tf_op jit(solution)/shard_map/all_to_all | solution.py:144
  361.4 13.9 %combine.3 = (f32[8,128,512]{2,1,0:T(8,128)}, f32[8,128,512]{2,1,0:T(8,128)}, bf16[16,128,512]{2,1,0:T(8,128)(2,1)}, bf16[16,128,512]{2,1,0:T(8,128)(2,1)}) custom-call(s32[16,2]{1,0:T(8,128)} %copy.19.share_ref, s32[8]{0:T(128)} %slot_ref.3, bf16[16,128,512]{2,1,0:T(8,128)(2,1)} %all-to-all-done.refs_0_, ...), custom_call_target="tpu_custom_call", output_to_operand_aliasing={{0}: (6, {}), {1}: (7, {})} | custom-call | flops 8388608 | bytes 16777216 | tf_op jit(solution)/shard_map/combine/pallas_call | solution.py:92
  375.4 12.9 %all-to-all-done.7 = bf16[16,128,512]{2,1,0:T(8,128)(2,1)S(1)} async-done(((bf16[16,128,512]{2,1,0:T(8,128)(2,1)}), bf16[16,128,512]{2,1,0:T(8,128)(2,1)S(1)}, u32[]{:S(2)}, u32[]{:S(2)}) %all-to-all-start.7) | async-done | bytes 2097184 | tf_op jit(solution)/shard_map/all_to_all | solution.py:144
  388.3 28.2 %all_to_all.41 = bf16[16,128,512]{2,1,0:T(8,128)(2,1)} all-to-all(bf16[16,128,512]{2,1,0:T(8,128)(2,1)} %get-tuple-element.18), channel_id=1, replica_groups=mesh['path'=16,'fsdp'=8] {'path'}, dimensions={0} | all-to-all | bytes 4194304 | tf_op jit(solution)/shard_map/all_to_all | solution.py:144
  420.3 5.8 %update.2 = (bf16[1,2,2048,512]{3,2,1,0:T(8,128)(2,1)}, bf16[1,2,2048,512]{3,2,1,0:T(8,128)(2,1)}) custom-call(bf16[1,2,2048,512]{3,2,1,0:T(8,128)(2,1)} %up_ref.3, bf16[1,2,2048,512]{3,2,1,0:T(8,128)(2,1)} %down_ref.3, bf16[2048,512]{1,0:T(8,128)(2,1)} %bitcast.64, bf16[2048,512]{1,0:T(8,128)(2,1)} %bitcast.65), custom_call_target="tpu_custom_call" | custom-call | flops 4194304 | bytes 12582912 | tf_op jit(solution)/shard_map/update/pallas_call | solution.py:129
  426.1 17.6 %all-to-all-done.5 = bf16[16,128,512]{2,1,0:T(8,128)(2,1)S(1)} async-done(((bf16[16,128,512]{2,1,0:T(8,128)(2,1)}), bf16[16,128,512]{2,1,0:T(8,128)(2,1)S(1)}, u32[]{:S(2)}, u32[]{:S(2)}) %all-to-all-start.5) | async-done | bytes 2097184 | tf_op jit(solution)/shard_map/all_to_all | solution.py:144
  445.0 5.8 %update.3 = (bf16[1,2,2048,512]{3,2,1,0:T(8,128)(2,1)}, bf16[1,2,2048,512]{3,2,1,0:T(8,128)(2,1)}) custom-call(bf16[1,2,2048,512]{3,2,1,0:T(8,128)(2,1)} %up_ref.3, bf16[1,2,2048,512]{3,2,1,0:T(8,128)(2,1)} %down_ref.3, bf16[2048,512]{1,0:T(8,128)(2,1)} %bitcast.61, bf16[2048,512]{1,0:T(8,128)(2,1)} %bitcast.62, ...), custom_call_target="tpu_custom_call", output_to_operand_aliasing={{0}: (4, {}), {1}: (5, {})} | custom-call | flops 4194304 | bytes 12582912 | tf_op jit(solution)/shard_map/update/pallas_call | solution.py:129
  (64 shorter events, 59.7 us)
Async XLA Ops:
  7.2 37.1 %all-gather.5.cloned.1.call-start = ((), (), s32[]{:S(2)}) async-start(), calls=%async_computation.10 | async-start | bytes 4718592 | tf_op jit(solution)/shard_map/all_gather | solution.py:168
  7.9 122.4 %all-reduce.3.cloned.1.call-start = ((), (), s32[]{:S(2)}) async-start(), calls=%async_computation.8 | async-start | bytes 8388608 | tf_op jit(solution)/shard_map/psum | solution.py:175
  47.7 5.5 %copy-start.7 = (bf16[1,2,2048,512]{3,2,1,0:T(8,128)(2,1)S(1)}, bf16[1,2,2048,512]{3,2,1,0:T(8,128)(2,1)}, u32[]{:S(2)}) copy-start(bf16[1,2,2048,512]{3,2,1,0:T(8,128)(2,1)} %down_ref.3) | copy-start | bytes 12582916
  57.9 106.3 %all-gather.7.cloned.1.call-start = ((), (), s32[]{:S(2)}) async-start(), calls=%async_computation.11 | async-start | bytes 4718592 | tf_op jit(solution)/shard_map/all_gather | solution.py:169
  130.3 5.0 %copy-start.1 = (bf16[1,1024,2048]{2,1,0:T(8,128)(2,1)S(1)}, bf16[1,1024,2048]{2,1,0:T(8,128)(2,1)}, u32[]{:S(2)}) copy-start(bf16[1,1024,2048]{2,1,0:T(8,128)(2,1)} %all-gather.5.cloned.1.call-done) | copy-start | bytes 12582916
  130.3 5.9 %copy-start.4 = (bf16[1024,2048]{1,0:T(8,128)(2,1)S(1)}, bf16[1024,2048]{1,0:T(8,128)(2,1)}, u32[]{:S(2)}) copy-start(bf16[1024,2048]{1,0:T(8,128)(2,1)} %all-reduce.3.cloned.1.call-done) | copy-start | bytes 12582916
  140.3 30.4 %copy-start.16 = (f32[1024,512]{1,0:T(8,128)}, f32[1024,512]{1,0:T(8,128)S(1)}, u32[]{:S(2)}) copy-start(f32[1024,512]{1,0:T(8,128)S(1)} %fusion.19) | copy-start | bytes 6291460
  164.2 6.5 %copy-start.2 = (bf16[1,1024,2048]{2,1,0:T(8,128)(2,1)S(1)}, bf16[1,1024,2048]{2,1,0:T(8,128)(2,1)}, u32[]{:S(2)}) copy-start(bf16[1,1024,2048]{2,1,0:T(8,128)(2,1)} %all-gather.5.cloned.1.call-done) | copy-start | bytes 12582916
  164.2 6.5 %copy-start.5 = (bf16[1024,2048]{1,0:T(8,128)(2,1)S(1)}, bf16[1024,2048]{1,0:T(8,128)(2,1)}, u32[]{:S(2)}) copy-start(bf16[1024,2048]{1,0:T(8,128)(2,1)} %all-reduce.3.cloned.1.call-done) | copy-start | bytes 12582916
  175.3 37.9 %all-to-all-start.2 = ((bf16[16,128,512]{2,1,0:T(8,128)(2,1)}), bf16[16,128,512]{2,1,0:T(8,128)(2,1)S(1)}, u32[]{:S(2)}, u32[]{:S(2)}) async-start(bf16[16,128,512]{2,1,0:T(8,128)(2,1)} %bitcast.66), calls=%async_computation.2 | async-start | bytes 4194304 | tf_op jit(solution)/shard_map/all_to_all | solution.py:144
  182.2 83.8 %all-reduce.5.cloned.1.call-start = ((), (), s32[]{:S(2)}) async-start(), calls=%async_computation.9 | async-start | bytes 8388608 | tf_op jit(solution)/shard_map/psum | solution.py:190
  213.2 6.0 %copy-start.15 = (s32[16,2]{0,1:T(2,128)S(1)}, s32[16,2]{0,1:T(2,128)}, u32[]{:S(2)}) copy-start(s32[16,2]{0,1:T(2,128)} %param.16) | copy-start | bytes 388
  214.6 33.5 %all-to-all-start.3 = ((bf16[16,128,512]{2,1,0:T(8,128)(2,1)}), bf16[16,128,512]{2,1,0:T(8,128)(2,1)}, u32[]{:S(2)}, u32[]{:S(2)}) async-start(bf16[16,128,512]{2,1,0:T(8,128)(2,1)} %bitcast.63), calls=%async_computation.3 | async-start | bytes 4194304 | tf_op jit(solution)/shard_map/all_to_all | solution.py:144
  262.1 31.5 %all-to-all-start.6 = ((bf16[16,128,512]{2,1,0:T(8,128)(2,1)}), bf16[16,128,512]{2,1,0:T(8,128)(2,1)S(1)}, u32[]{:S(2)}, u32[]{:S(2)}) async-start(bf16[16,128,512]{2,1,0:T(8,128)(2,1)} %get-tuple-element.20), calls=%async_computation.6 | async-start | bytes 4194304 | tf_op jit(solution)/shard_map/all_to_all | solution.py:144
  266.0 6.8 %copy-start.3 = (bf16[1,1024,2048]{2,1,0:T(8,128)(2,1)S(1)}, bf16[1,1024,2048]{2,1,0:T(8,128)(2,1)}, u32[]{:S(2)}) copy-start(bf16[1,1024,2048]{2,1,0:T(8,128)(2,1)} %all-gather.5.cloned.1.call-done) | copy-start | bytes 12582916
  266.0 7.1 %copy-start.6 = (bf16[1024,2048]{1,0:T(8,128)(2,1)S(1)}, bf16[1024,2048]{1,0:T(8,128)(2,1)}, u32[]{:S(2)}) copy-start(bf16[1024,2048]{1,0:T(8,128)(2,1)} %all-reduce.3.cloned.1.call-done) | copy-start | bytes 12582916
  266.0 8.3 %copy-start.9 = (bf16[1024,2048]{1,0:T(8,128)(2,1)S(1)}, bf16[1024,2048]{1,0:T(8,128)(2,1)}, u32[]{:S(2)}) copy-start(bf16[1024,2048]{1,0:T(8,128)(2,1)} %all-reduce.5.cloned.1.call-done) | copy-start | bytes 12582916
  274.3 6.9 %copy-start.8 = (bf16[1,2,2048,512]{3,2,1,0:T(8,128)(2,1)S(1)}, bf16[1,2,2048,512]{3,2,1,0:T(8,128)(2,1)}, u32[]{:S(2)}) copy-start(bf16[1,2,2048,512]{3,2,1,0:T(8,128)(2,1)} %down_ref.3) | copy-start | bytes 12582916
  274.3 6.9 %copy-start.18 = (f32[1024,512]{1,0:T(8,128)S(1)}, f32[1024,512]{1,0:T(8,128)}, u32[]{:S(2)}) copy-start(f32[1024,512]{1,0:T(8,128)} %copy-done.17) | copy-start | bytes 6291460
  281.2 3.5 copy-start.14
  295.0 32.3 %all-to-all-start = ((bf16[16,128,512]{2,1,0:T(8,128)(2,1)}), bf16[16,128,512]{2,1,0:T(8,128)(2,1)}, u32[]{:S(2)}, u32[]{:S(2)}) async-start(bf16[16,128,512]{2,1,0:T(8,128)(2,1)} %bitcast.67), calls=%async_computation | async-start | bytes 4194304 | tf_op jit(solution)/shard_map/all_to_all | solution.py:144
  357.7 30.6 %all-to-all-start.7 = ((bf16[16,128,512]{2,1,0:T(8,128)(2,1)}), bf16[16,128,512]{2,1,0:T(8,128)(2,1)S(1)}, u32[]{:S(2)}, u32[]{:S(2)}) async-start(bf16[16,128,512]{2,1,0:T(8,128)(2,1)} %get-tuple-element.21), calls=%async_computation.7 | async-start | bytes 4194304 | tf_op jit(solution)/shard_map/all_to_all | solution.py:144
  388.3 28.2 %copy-start.13 = (bf16[16,128,512]{2,1,0:T(8,128)(2,1)}, bf16[16,128,512]{2,1,0:T(8,128)(2,1)S(1)}, u32[]{:S(2)}) copy-start(bf16[16,128,512]{2,1,0:T(8,128)(2,1)S(1)} %all-to-all-done.7) | copy-start | bytes 6291460
  416.5 27.2 %all-to-all-start.5 = ((bf16[16,128,512]{2,1,0:T(8,128)(2,1)}), bf16[16,128,512]{2,1,0:T(8,128)(2,1)S(1)}, u32[]{:S(2)}, u32[]{:S(2)}) async-start(bf16[16,128,512]{2,1,0:T(8,128)(2,1)} %get-tuple-element.19), calls=%async_computation.5 | async-start | bytes 4194304 | tf_op jit(solution)/shard_map/all_to_all | solution.py:144
  (5 other events, 8.9 us)
Sparse Core Ops, SparseCore 0:
  9.7 34.5 all-gather.4
  58.0 72.2 all-reduce.2
  132.0 32.1 all-gather.6
  188.9 73.0 all-reduce.4

commit v2 on v1

v2 whole, which is shorter than its diff:
```python
import functools
import math

import jax
import jax.numpy as jnp
from jax import lax
from jax.experimental import pallas as pl
from jax.experimental.pallas import tpu as pltpu
from jax.sharding import PartitionSpec as P

PER_LEVEL = 4

epsilon = 1e-06
gelu_coef = 0.7978845608
cubic_coef = 0.044715
momentum_decay = 0.9
outer_rate = 0.7


def gelu_tanh(value):
    inner = gelu_coef * (value + cubic_coef * value * value * value)
    return 0.5 * value * (1.0 + jnp.tanh(inner))


def gelu_slope(value):
    inner = gelu_coef * (value + cubic_coef * value * value * value)
    tangent = jnp.tanh(inner)
    return 0.5 * (1.0 + tangent) + 0.5 * value * (1.0 - tangent * tangent) * gelu_coef * (
        1.0 + 3.0 * cubic_coef * value * value
    )


def rms_norm(rows, gain):
    return rows * lax.rsqrt(jnp.mean(rows * rows, axis=-1, keepdims=True) + epsilon) * gain


def norm_back(rows, gain, upstream):
    _, pull = jax.vjp(lambda inner_rows: rms_norm(inner_rows, gain), rows)
    return pull(upstream)[0]


def contract_last(left, right):
    return lax.dot_general(
        left, right, (((1,), (1,)), ((), ())), preferred_element_type=jnp.float32
    )


def contract_first(left, right):
    return lax.dot_general(
        left, right, (((0,), (0,)), ((), ())), preferred_element_type=jnp.float32
    )


def combine_body(level, paths, share_ref, slot_ref, recv, mom, *refs):
    out, send, acc = refs[-3:]
    module = pl.program_id(1)
    acc[...] = jnp.zeros_like(acc)
    count = jnp.float32(0.0)
    for path in range(paths):
        hit = share_ref[path, level] == module
        count = count + jnp.where(hit, 1.0, 0.0)

        @pl.when(hit)
        def _():
            acc[...] += recv[path].astype(jnp.float32)

    divisor = jnp.full((1, acc.shape[1]), jnp.maximum(count, 1.0), jnp.float32)
    pseudo = acc[...] * (1.0 / divisor)
    fresh = momentum_decay * mom[0] + pseudo
    out[0] = fresh
    acc[...] = pseudo + momentum_decay * fresh
    for path in range(paths):

        @pl.when(share_ref[path, level] == module)
        def _():
            send[path] = acc[...].astype(jnp.bfloat16)


def combine(level, share, slots, recv, mom, partial):
    paths, rows, cols = recv.shape
    step = 32
    mom_spec = pl.BlockSpec(
        (1, step, cols), lambda r, m, share, slots: (slots[level * PER_LEVEL + m], r, 0)
    )
    path_spec = pl.BlockSpec((paths, step, cols), lambda r, m, share, slots: (0, r, 0))
    hold = [pl.BlockSpec(memory_space=pl.ANY)] * len(partial)
    return pl.pallas_call(
        functools.partial(combine_body, level, paths),
        grid_spec=pltpu.PrefetchScalarGridSpec(
            num_scalar_prefetch=2,
            grid=(rows // step, PER_LEVEL),
            in_specs=[path_spec, mom_spec] + hold,
            out_specs=[mom_spec, path_spec],
            scratch_shapes=[pltpu.VMEM((step, cols), jnp.float32)],
        ),
        out_shape=[
            jax.ShapeDtypeStruct(mom.shape, jnp.float32),
            jax.ShapeDtypeStruct(recv.shape, jnp.bfloat16),
        ],
        input_output_aliases={4: 0} if partial else {},
        cost_estimate=pl.CostEstimate(
            flops=4 * recv.size, bytes_accessed=8 * recv.size, transcendentals=0
        ),
        name="combine",
    )(share, slots, recv, mom, *partial)


def update_body(old, back, *refs):
    new = refs[-1]
    new[0, 0] = (
        old[0, 0].astype(jnp.float32) - outer_rate * back[...].astype(jnp.float32)
    ).astype(jnp.bfloat16)


def update(level, proj, back, partial):
    _, _, rows, cols = proj.shape
    step = 512
    full = pl.BlockSpec((1, 1, step, cols), lambda r: (0, level, r, 0))
    flat = pl.BlockSpec((step, cols), lambda r: (r, 0))
    hold = [pl.BlockSpec(memory_space=pl.ANY)] * len(partial)
    return pl.pallas_call(
        update_body,
        grid=(rows // step,),
        in_specs=[full, flat] + hold,
        out_specs=full,
        out_shape=jax.ShapeDtypeStruct(proj.shape, proj.dtype),
        input_output_aliases={2: 0} if partial else {},
        cost_estimate=pl.CostEstimate(
            flops=2 * rows * cols, bytes_accessed=6 * rows * cols, transcendentals=0
        ),
        name="update",
    )(proj, back.reshape(rows, cols), *partial)


def cube():
    place = lax.axis_index("fsdp")
    row, core = place // 2, place % 2
    across = row + 1 - 2 * (row % 2)
    return row, core, across, 3 - row, (row + 2) % 4


def greet(peers):
    barrier = pltpu.get_barrier_semaphore()
    for peer in peers:
        pl.semaphore_signal(
            barrier, inc=1, device_id={"fsdp": peer}, device_id_type=pl.DeviceIdType.MESH
        )
    pl.semaphore_wait(barrier, len(peers))


def gather_body(own, out, send_sem, recv_sem, local_sem):
    row, core, row_a, row_b, row_d = cube()
    me, sibling = row * 2 + core, row * 2 + 1 - core
    peer_a, peer_b, block_d = row_a * 2 + core, row_b * 2 + core, row_d * 2 + core
    greet((sibling, peer_a, peer_b))
    half = own.shape[0] // 2
    parts = (pl.ds(0, half), pl.ds(half, half))

    def copy(index, source, block, part, peer):
        return pltpu.make_async_remote_copy(
            src_ref=source,
            dst_ref=out.at[block, part],
            send_sem=send_sem.at[index],
            recv_sem=recv_sem.at[index],
            device_id={"fsdp": peer},
            device_id_type=pl.DeviceIdType.MESH,
        )

    whole = pl.ds(0, own.shape[0])
    first, second = parts
    a_second = copy(0, own.at[second], me, second, peer_a)
    b_first = copy(1, own.at[first], me, first, peer_b)
    a_first = copy(2, own.at[first], me, first, peer_a)
    b_second = copy(3, own.at[second], me, second, peer_b)
    mine = copy(4, own, me, whole, sibling)
    stay = pltpu.make_async_copy(own, out.at[me], local_sem)
    for step in (a_second, b_first, a_first, b_second, mine, stay):
        step.start()

    def relay(index, block, part, peer):
        return copy(index, out.at[block, part], block, part, peer)

    b_first.wait_recv()
    onward_a = relay(5, peer_b, first, peer_a)
    onward_a.start()
    a_second.wait_recv()
    onward_b = relay(6, peer_a, second, peer_b)
    onward_b.start()
    side = [relay(7, peer_b, first, sibling), relay(8, peer_a, second, sibling)]
    for step in side:
        step.start()
    a_first.wait_recv()
    side.append(relay(9, peer_a, first, sibling))
    side[-1].start()
    b_second.wait_recv()
    side.append(relay(10, peer_b, second, sibling))
    side[-1].start()
    onward_a.wait_recv()
    side.append(relay(11, block_d, first, sibling))
    side[-1].start()
    onward_b.wait_recv()
    side.append(relay(12, block_d, second, sibling))
    side[-1].start()
    mine.wait_recv()
    for step in side:
        step.wait_recv()
    stay.wait()
    for step in (a_second, b_first, a_first, b_second, mine, onward_a, onward_b, *side):
        step.wait_send()


def gather(own, collective):
    rows, cols = own.shape
    return pl.pallas_call(
        gather_body,
        in_specs=[pl.BlockSpec(memory_space=pltpu.VMEM)],
        out_specs=pl.BlockSpec(memory_space=pl.ANY),
        out_shape=jax.ShapeDtypeStruct((8, rows, cols), own.dtype),
        scratch_shapes=[
            pltpu.SemaphoreType.DMA((13,)),
            pltpu.SemaphoreType.DMA((13,)),
            pltpu.SemaphoreType.DMA,
        ],
        compiler_params=pltpu.CompilerParams(collective_id=collective, has_side_effects=True),
        cost_estimate=pl.CostEstimate(flops=0, bytes_accessed=60 * 2**20, transcendentals=0),
        name="gather",
    )(own).reshape(8 * rows, cols)


def scatter_body(parts_ref, out, near, summed, first_in, second_in, send_sem, recv_sem):
    row, core, row_a, row_b, row_d = cube()
    sibling = row * 2 + 1 - core
    peer_a, peer_b = row_a * 2 + core, row_b * 2 + core
    greet((sibling, peer_a, peer_b))
    half = out.shape[0] // 2
    top, low = pl.ds(0, half), pl.ds(half, half)
    order = (row_d, row_a, row_b, row)

    def copy(index, source, target, peer):
        return pltpu.make_async_remote_copy(
            src_ref=source,
            dst_ref=target,
            send_sem=send_sem.at[index],
            recv_sem=recv_sem.at[index],
            device_id={"fsdp": peer},
            device_id_type=pl.DeviceIdType.MESH,
        )

    swaps = [
        copy(k, parts_ref.at[order[k] * 2 + 1 - core], near.at[k], sibling) for k in range(4)
    ]
    for step in swaps:
        step.start()

    def settle(k):
        swaps[k].wait_recv()
        mine = parts_ref[order[k] * 2 + core].astype(jnp.float32)
        summed[k] = (mine + near[k].astype(jnp.float32)).astype(jnp.bfloat16)

    settle(0)
    settle(1)
    far_a = copy(4, summed.at[0, top], first_in.at[0], peer_a)
    far_b = copy(5, summed.at[0, low], first_in.at[1], peer_b)
    far_a.start()
    far_b.start()
    settle(2)
    near_a = copy(6, summed.at[1, top], first_in.at[2], peer_a)
    near_a.start()
    settle(3)
    near_b = copy(7, summed.at[2, low], first_in.at[3], peer_b)
    near_b.start()
    far_a.wait_recv()
    second_in[0] = (
        summed[2, top].astype(jnp.float32) + first_in[0].astype(jnp.float32)
    ).astype(jnp.bfloat16)
    far_b.wait_recv()
    second_in[1] = (
        summed[1, low].astype(jnp.float32) + first_in[1].astype(jnp.float32)
    ).astype(jnp.bfloat16)
    last_b = copy(8, second_in.at[0], second_in.at[2], peer_b)
    last_b.start()
    near_a.wait_recv()
    out[top] = summed[3, top].astype(jnp.float32) + first_in[2].astype(jnp.float32)
    last_a = copy(9, second_in.at[1], second_in.at[3], peer_a)
    last_a.start()
    near_b.wait_recv()
    out[low] = summed[3, low].astype(jnp.float32) + first_in[3].astype(jnp.float32)
    last_b.wait_recv()
    out[top] += second_in[2].astype(jnp.float32)
    last_a.wait_recv()
    out[low] += second_in[3].astype(jnp.float32)
    for step in (*swaps, far_a, far_b, near_a, near_b, last_a, last_b):
        step.wait_send()


def scatter(parts, collective):
    rows, cols = parts.shape
    rows = rows // 8
    return pl.pallas_call(
        scatter_body,
        in_specs=[pl.BlockSpec(memory_space=pltpu.VMEM)],
        out_specs=pl.BlockSpec(memory_space=pltpu.VMEM),
        out_shape=jax.ShapeDtypeStruct((rows, cols), jnp.float32),
        scratch_shapes=[
            pltpu.VMEM((4, rows, cols), jnp.bfloat16),
            pltpu.VMEM((4, rows, cols), jnp.bfloat16),
            pltpu.VMEM((4, rows // 2, cols), jnp.bfloat16),
            pltpu.VMEM((4, rows // 2, cols), jnp.bfloat16),
            pltpu.SemaphoreType.DMA((10,)),
            pltpu.SemaphoreType.DMA((10,)),
        ],
        compiler_params=pltpu.CompilerParams(collective_id=collective, has_side_effects=True),
        cost_estimate=pl.CostEstimate(flops=0, bytes_accessed=70 * 2**20, transcendentals=0),
        name="scatter",
    )(parts.reshape(8, rows, cols))


def swap(value):
    return lax.all_to_all(value, "path", split_axis=0, concat_axis=0, tiled=True)


def shards(
    tokens, cotangent, norm_gain, up_proj, down_proj, mom_up, mom_down, share_table, module_slot
):
    scale_in = 1.0 / math.sqrt(2048)
    scale_out = 1.0 / math.sqrt(4096)
    norm_gains = norm_gain[0]
    up_local = up_proj[0]
    down_local = down_proj[0]
    paths = share_table.shape[0]
    row_block, col_block = mom_up.shape[1:]

    def blocks(grad):
        return grad.astype(jnp.bfloat16).reshape(paths, row_block, col_block)

    def merge(level, recv, mom, partial):
        return combine(level, share_table, module_slot, recv, mom, partial)

    tie = lax.optimization_barrier

    cot_all = lax.all_gather(cotangent[0], "fsdp", axis=0, tiled=True)
    tok_float = tokens[0].astype(jnp.float32)
    first_normed = gather(rms_norm(tok_float, norm_gains[0]).astype(jnp.bfloat16), 0)
    first_pre = jnp.dot(first_normed, up_local[0], preferred_element_type=jnp.float32) * scale_in
    first_hidden = gelu_tanh(first_pre).astype(jnp.bfloat16)
    second_input = tok_float + scatter(
        (contract_last(first_hidden, down_local[0]) * scale_out).astype(jnp.bfloat16), 1
    )
    second_normed = gather(rms_norm(second_input, norm_gains[1]).astype(jnp.bfloat16), 2)
    second_pre = jnp.dot(second_normed, up_local[1], preferred_element_type=jnp.float32) * scale_in
    second_hidden = gelu_tanh(second_pre).astype(jnp.bfloat16)
    grad_down_upper = contract_first(cot_all, second_hidden) * scale_out
    recv_down_1 = swap(blocks(grad_down_upper))
    second_slope = (
        jnp.dot(cot_all, down_local[1], preferred_element_type=jnp.float32)
        * scale_out
        * gelu_slope(second_pre)
    ).astype(jnp.bfloat16)
    grad_up_upper = contract_first(second_normed, second_slope) * scale_in
    back_parts = (contract_last(second_slope, up_local[1]) * scale_in).astype(jnp.bfloat16)
    grad_up_upper, recv_down_1, back_parts = tie(
        (blocks(grad_up_upper), recv_down_1, back_parts)
    )
    recv_up_1 = swap(grad_up_upper)
    back_summed = scatter(back_parts, 3)
    own_grad = (
        cotangent[0].astype(jnp.float32) + norm_back(second_input, norm_gains[1], back_summed)
    ).astype(jnp.bfloat16)
    mom_down_1, send_down_1 = merge(1, recv_down_1, mom_down, ())
    own_grad, send_down_1, recv_up_1 = tie((own_grad, send_down_1, recv_up_1))
    back_down_1 = swap(send_down_1)
    first_grad, back_down_1 = tie((gather(own_grad, 4), back_down_1))
    grad_down_lower = contract_first(first_grad, first_hidden) * scale_out
    first_slope = (
        jnp.dot(first_grad, down_local[0], preferred_element_type=jnp.float32)
        * scale_out
        * gelu_slope(first_pre)
    ).astype(jnp.bfloat16)
    grad_up_lower = contract_first(first_normed, first_slope) * scale_in
    mom_up_1, send_up_1 = merge(1, recv_up_1, mom_up, ())
    recv_down_0 = swap(blocks(grad_down_lower))
    grad_up_lower, recv_down_0 = tie((blocks(grad_up_lower), recv_down_0))
    recv_up_0 = swap(grad_up_lower)
    new_mom_down, send_down_0 = merge(0, recv_down_0, mom_down, (mom_down_1,))
    send_up_1, recv_up_0 = tie((send_up_1, recv_up_0))
    back_up_1 = swap(send_up_1)
    new_mom_up, send_up_0 = merge(0, recv_up_0, mom_up, (mom_up_1,))
    send_down_0, back_up_1 = tie((send_down_0, back_up_1))
    back_down_0 = swap(send_down_0)
    send_up_0, back_down_0 = tie((send_up_0, back_down_0))
    back_up_0 = swap(send_up_0)
    down_1 = update(1, down_proj, back_down_1, ())
    up_1 = update(1, up_proj, back_up_1, ())
    new_down = update(0, down_proj, back_down_0, (down_1,))
    new_up = update(0, up_proj, back_up_0, (up_1,))
    return (new_up, new_down, new_mom_up, new_mom_down)


def solution(mesh):
    in_specs = (
        P("path", "fsdp", None),
        P("path", "fsdp", None),
        P("path", None, None),
        P("path", None, None, "fsdp"),
        P("path", None, None, "fsdp"),
        P(None, "path", "fsdp"),
        P(None, "path", "fsdp"),
        P(),
        P(),
    )
    out_specs = (
        P("path", None, None, "fsdp"),
        P("path", None, None, "fsdp"),
        P(None, "path", "fsdp"),
        P(None, "path", "fsdp"),
    )
    return jax.shard_map(shards, mesh=mesh, in_specs=in_specs, out_specs=out_specs, check_vma=False)
```

time: 464 us -> 439 us (0.946)
  Pallas kernels: 39.5 us -> 205 us
  waiting for transfers between devices: 232 us -> 99.2 us
  blocking collectives: 58.6 us -> 0 us
  other arithmetic: 21.9 us -> 7.31 us
  starting transfers between devices: 28.4 us -> 42.8 us
  matrix products: 49.6 us -> 56.8 us
    pallas_call x2 -> x9, Pallas kernels: 11.6 us -> 156 us  [the longest x3 80 us: gather(): pl.pallas_call(gather_body, in_specs=[pl.BlockSpec(memory_space=pltpu.VME...]
    psum x2 -> x0, waiting for transfers between devices: 71.7 us -> none  [the longest x1 71.7 us: shards(): lax.psum((contract_last(first_hidden, down_local[0]) * scale_out).astype(...]
    all_gather x2 -> x1, waiting for transfers between devices: 59.4 us -> 0.01 us  [shards(): cot_all = lax.all_gather(cotangent[0], 'fsdp', axis=0, tiled=True)]
    all_to_all x2 -> x0, blocking collectives: 58.6 us -> none  [swap(): lax.all_to_all(value, 'path', split_axis=0, concat_axis=0, tiled=True)]
    pallas_call x2 -> x4, Pallas kernels: 28 us -> 49.6 us  [combine(): pl.pallas_call(functools.partial(combine_body, level, paths), grid_spec=p...]
    all_to_all x6 -> x8, starting transfers between devices: 27.5 us -> 42.8 us  [swap(): lax.all_to_all(value, 'path', split_axis=0, concat_axis=0, tiled=True)]
    reduce_sum x1, other arithmetic: 6.76 us -> 0.29 us  [rms_norm(): rows * lax.rsqrt(jnp.mean(rows * rows, axis=-1, keepdims=True) + epsilon)]
    reduce_sum x2, other arithmetic: 8.24 us -> 2.76 us  [rms_norm(): jnp.mean(rows * rows, axis=-1, keepdims=True) + epsilon]
  transfers between devices with their start and end apart: 10 -> 9, of which waited for: 9 -> 7; matrix products, arithmetic and copies ran while one was open for 12% -> 12% of each run, Pallas kernels for 7% -> 46%
where the time goes in v2:
time: 439 us; the launch traced here: 436 us
  Pallas kernels  205 us (47%)
  waiting for transfers between devices  99.2 us (23%)
  matrix products  56.8 us (13%)
  starting transfers between devices  42.8 us (10%)
  between operations  14.3 us (3%)
  local copies, waits for them, and re-layouts  10.2 us (2%)
  other arithmetic  7.31 us (2%)
    all_to_all x8, waiting for transfers between devices, swap(): lax.all_to_all(value, 'path', split_axis=0, concat_axis=0, tiled=True)  98.5 us
    pallas_call x3, Pallas kernels, gather(): pl.pallas_call(gather_body, in_specs=[pl.BlockSpec(memory_space=pltpu.VME...  80 us
    pallas_call x2, Pallas kernels, scatter(): pl.pallas_call(scatter_body, in_specs=[pl.BlockSpec(memory_space=pltpu.VM...  58.1 us
    pallas_call x4, Pallas kernels, combine(): pl.pallas_call(functools.partial(combine_body, level, paths), grid_spec=p...  49.6 us
    all_to_all x8, starting transfers between devices, swap(): lax.all_to_all(value, 'path', split_axis=0, concat_axis=0, tiled=True)  42.8 us
    dot_general x4, matrix products, contract_first(): lax.dot_general(left, right, (((0,), (0,)), ((), ())), preferred_element_...  21.7 us
    pallas_call x4, Pallas kernels, update(): pl.pallas_call(update_body, grid=(rows // step,), in_specs=[full, flat] +...  17.5 us
    dot_general x2, matrix products, contract_last(): lax.dot_general(left, right, (((1,), (1,)), ((), ())), preferred_element_...  9.08 us
  transfers between devices with their start and end apart: 9, of which 7 were waited for; matrix products, arithmetic and copies ran while one was open for 12% of the time, Pallas kernels for 46%

profile of v2, /device:TPU:0, one launch (start us, length us, event | category | flops | bytes accessed | tf_op | source)
XLA Modules:
  0.0 435.8 jit_solution(12022582273515083714)
XLA Ops:
  12.0 33.7 %gather.3 = bf16[8,128,2048]{2,1,0:T(8,128)(2,1)} custom-call(bf16[128,2048]{1,0:T(8,128)(2,1)} %fusion.40.own), custom_call_target="tpu_custom_call" | custom-call | bytes 62914560 | tf_op jit(solution)/shard_map/gather/pallas_call | solution.py:214
  45.7 5.5 %fusion.20 = f32[1024,512]{1,0:T(8,128)S(1)} fusion(bf16[1024,2048]{1,0:T(8,128)(2,1)} %bitcast.79, bf16[1,2,2048,512]{3,2,1,0:T(8,128)(2,1)} %old.5), kind=kOutput, calls=%fused_computation.24 | convolution fusion | flops 2147483648 | bytes 8388608 | tf_op jit(solution)/shard_map/dot_general | solution.py:344
  55.8 31.0 %scatter.2 = f32[128,2048]{1,0:T(8,128)} custom-call(bf16[8,128,2048]{2,1,0:T(8,128)(2,1)} %bitcast.78), custom_call_target="tpu_custom_call" | custom-call | bytes 73400320 | tf_op jit(solution)/shard_map/scatter/pallas_call | solution.py:299
  89.4 22.8 %gather.4 = bf16[8,128,2048]{2,1,0:T(8,128)(2,1)} custom-call(bf16[128,2048]{1,0:T(8,128)(2,1)} %multiply_convert_fusion.11.own), custom_call_target="tpu_custom_call" | custom-call | bytes 62914560 | tf_op jit(solution)/shard_map/gather/pallas_call | solution.py:214
  112.2 6.5 %fusion.14 = f32[1024,512]{1,0:T(8,128)} fusion(bf16[1024,2048]{1,0:T(8,128)(2,1)} %bitcast.81, bf16[1,2,2048,512]{3,2,1,0:T(8,128)(2,1)} %old.5), kind=kOutput, calls=%fused_computation.18 | convolution fusion | flops 2147483648 | bytes 8388608 | tf_op jit(solution)/shard_map/dot_general | solution.py:350
  118.7 6.7 %fusion.6 = bf16[2048,512]{0,1:T(8,128)(2,1)} fusion(bf16[1,1024,2048]{2,1,0:T(8,128)(2,1)} %all-gather.3.cloned.1.call-done, f32[1024,512]{1,0:T(8,128)} %fusion.14), kind=kOutput, calls=%fused_computation.12 | convolution fusion | flops 2154823680 | bytes 8388608 | tf_op jit(solution)/shard_map/dot_general | solution.py:49
  129.3 8.8 %all-to-all-start = ((bf16[16,128,512]{2,1,0:T(8,128)(2,1)}), bf16[16,128,512]{2,1,0:T(8,128)(2,1)}, u32[]{:S(2)}, u32[]{:S(2)}) async-start(bf16[16,128,512]{2,1,0:T(8,128)(2,1)} %bitcast.76), calls=%async_computation | async-start | bytes 4194304 | tf_op jit(solution)/shard_map/all_to_all | solution.py:319
  138.2 7.0 %multiply_convert_fusion.8 = bf16[1024,512]{1,0:T(8,128)(2,1)S(1)} fusion(f32[1024,512]{1,0:T(8,128)} %fusion.14, bf16[1,2,2048,512]{3,2,1,0:T(8,128)(2,1)} %old.7, bf16[1,1024,2048]{2,1,0:T(8,128)(2,1)} %all-gather.3.cloned.1.call-done), kind=kOutput, calls=%fused_computation.28 | convolution fusion | flops 2158493696 | bytes 9437184 | tf_op jit(solution)/shard_map/dot_general | solution.py:355
  153.5 15.5 %all-to-all-done.recv = bf16[16,128,512]{2,1,0:T(8,128)(2,1)} async-done(((bf16[16,128,512]{2,1,0:T(8,128)(2,1)}), bf16[16,128,512]{2,1,0:T(8,128)(2,1)}, u32[]{:S(2)}, u32[]{:S(2)}) %all-to-all-start) | async-done | bytes 2097184 | tf_op jit(solution)/shard_map/all_to_all | solution.py:319
  174.8 27.1 %scatter.3 = f32[128,2048]{1,0:T(8,128)} custom-call(bf16[8,128,2048]{2,1,0:T(8,128)(2,1)} %bitcast.77), custom_call_target="tpu_custom_call" | custom-call | bytes 73400320 | tf_op jit(solution)/shard_map/scatter/pallas_call | solution.py:299
  202.0 12.5 %combine.4 = (f32[8,128,512]{2,1,0:T(8,128)}, bf16[16,128,512]{2,1,0:T(8,128)(2,1)}) custom-call(s32[16,2]{1,0:T(8,128)} %copy.20.share_ref, s32[8]{0:T(128)} %slot_ref.7, bf16[16,128,512]{2,1,0:T(8,128)(2,1)} %all-to-all-done.recv, f32[8,128,512]{2,1,0:T(8,128)} %mom.7), custom_call_target="tpu_custom_call" | custom-call | flops 4194304 | bytes 8388608 | tf_op jit(solution)/shard_map/combine/pallas_call | solution.py:87
  216.7 7.1 %all-to-all-start.2 = ((bf16[16,128,512]{2,1,0:T(8,128)(2,1)}), bf16[16,128,512]{2,1,0:T(8,128)(2,1)S(1)}, u32[]{:S(2)}, u32[]{:S(2)}) async-start(bf16[16,128,512]{2,1,0:T(8,128)(2,1)} %get-tuple-element.35), calls=%async_computation.2 | async-start | bytes 4194304 | tf_op jit(solution)/shard_map/all_to_all | solution.py:319
  223.8 23.5 %gather.5 = bf16[8,128,2048]{2,1,0:T(8,128)(2,1)} custom-call(bf16[128,2048]{1,0:T(8,128)(2,1)} %fusion.37.own), custom_call_target="tpu_custom_call" | custom-call | bytes 62914560 | tf_op jit(solution)/shard_map/gather/pallas_call | solution.py:214
  247.3 7.7 %all-to-all-done.2 = bf16[16,128,512]{2,1,0:T(8,128)(2,1)S(1)} async-done(((bf16[16,128,512]{2,1,0:T(8,128)(2,1)}), bf16[16,128,512]{2,1,0:T(8,128)(2,1)S(1)}, u32[]{:S(2)}, u32[]{:S(2)}) %all-to-all-start.2) | async-done | bytes 2097184 | tf_op jit(solution)/shard_map/all_to_all | solution.py:319
  255.0 7.5 %multiply_convert_fusion.2 = bf16[2048,512]{1,0:T(8,128)(2,1)} fusion(bf16[1024,2048]{1,0:T(8,128)(2,1)} %bitcast.83, f32[1024,512]{1,0:T(8,128)} %copy-done.13), kind=kOutput, calls=%fused_computation.6 | convolution fusion | flops 2154823680 | bytes 8388608 | tf_op jit(solution)/shard_map/dot_general | solution.py:49
  266.3 7.0 %multiply_convert_fusion.6 = bf16[1024,512]{1,0:T(8,128)(2,1)S(1)} fusion(f32[1024,512]{1,0:T(8,128)} %copy-done.13, bf16[1024,2048]{1,0:T(8,128)(2,1)} %bitcast.84, bf16[1,2,2048,512]{3,2,1,0:T(8,128)(2,1)} %old.7), kind=kOutput, calls=%fused_computation.26 | convolution fusion | flops 2158493696 | bytes 9437184 | tf_op jit(solution)/shard_map/dot_general | solution.py:375
  277.1 17.9 %all-to-all-done.3.recv = bf16[16,128,512]{2,1,0:T(8,128)(2,1)S(1)} async-done(((bf16[16,128,512]{2,1,0:T(8,128)(2,1)}), bf16[16,128,512]{2,1,0:T(8,128)(2,1)S(1)}, u32[]{:S(2)}, u32[]{:S(2)}) %all-to-all-start.3) | async-done | bytes 2097184 | tf_op jit(solution)/shard_map/all_to_all | solution.py:319
  300.7 12.4 %combine.5 = (f32[8,128,512]{2,1,0:T(8,128)}, bf16[16,128,512]{2,1,0:T(8,128)(2,1)}) custom-call(s32[16,2]{1,0:T(8,128)} %copy.20.share_ref, s32[8]{0:T(128)} %slot_ref.7, bf16[16,128,512]{2,1,0:T(8,128)(2,1)} %all-to-all-done.1.recv, f32[8,128,512]{2,1,0:T(8,128)} %mom.6), custom_call_target="tpu_custom_call" | custom-call | flops 4194304 | bytes 8388608 | tf_op jit(solution)/shard_map/combine/pallas_call | solution.py:87
  313.1 14.7 %all-to-all-done.4.recv = bf16[16,128,512]{2,1,0:T(8,128)(2,1)} async-done(((bf16[16,128,512]{2,1,0:T(8,128)(2,1)}), bf16[16,128,512]{2,1,0:T(8,128)(2,1)}, u32[]{:S(2)}, u32[]{:S(2)}) %all-to-all-start.4) | async-done | bytes 2097184 | tf_op jit(solution)/shard_map/all_to_all | solution.py:319
  332.6 12.4 %combine.7 = (f32[8,128,512]{2,1,0:T(8,128)}, bf16[16,128,512]{2,1,0:T(8,128)(2,1)}) custom-call(s32[16,2]{1,0:T(8,128)} %copy.20.share_ref, s32[8]{0:T(128)} %slot_ref.7, bf16[16,128,512]{2,1,0:T(8,128)(2,1)} %copy-done.8, f32[8,128,512]{2,1,0:T(8,128)} %mom.7, f32[8,128,512]{2,1,0:T(8,128)} %get-tuple-element.42.refs_0_), custom_call_target="tpu_custom_call", output_to_operand_aliasing={{0}: (4, {})} | custom-call | flops 4194304 | bytes 8388608 | tf_op jit(solution)/shard_map/combine/pallas_call | solution.py:87
  344.9 12.8 %all-to-all-done.5 = bf16[16,128,512]{2,1,0:T(8,128)(2,1)S(1)} async-done(((bf16[16,128,512]{2,1,0:T(8,128)(2,1)}), bf16[16,128,512]{2,1,0:T(8,128)(2,1)S(1)}, u32[]{:S(2)}, u32[]{:S(2)}) %all-to-all-start.5) | async-done | bytes 2097184 | tf_op jit(solution)/shard_map/all_to_all | solution.py:319
  363.5 12.4 %combine.6 = (f32[8,128,512]{2,1,0:T(8,128)}, bf16[16,128,512]{2,1,0:T(8,128)(2,1)}) custom-call(s32[16,2]{1,0:T(8,128)} %copy.20.share_ref, s32[8]{0:T(128)} %slot_ref.7, bf16[16,128,512]{2,1,0:T(8,128)(2,1)} %all-to-all-done.4.recv, f32[8,128,512]{2,1,0:T(8,128)} %mom.6, f32[8,128,512]{2,1,0:T(8,128)} %get-tuple-element.39.refs_0_), custom_call_target="tpu_custom_call", output_to_operand_aliasing={{0}: (4, {})} | custom-call | flops 4194304 | bytes 8388608 | tf_op jit(solution)/shard_map/combine/pallas_call | solution.py:87
  375.9 15.4 %all-to-all-done.6 = bf16[16,128,512]{2,1,0:T(8,128)(2,1)} async-done(((bf16[16,128,512]{2,1,0:T(8,128)(2,1)}), bf16[16,128,512]{2,1,0:T(8,128)(2,1)}, u32[]{:S(2)}, u32[]{:S(2)}) %all-to-all-start.6) | async-done | bytes 2097184 | tf_op jit(solution)/shard_map/all_to_all | solution.py:319
  408.6 14.7 %all-to-all-done.7 = bf16[16,128,512]{2,1,0:T(8,128)(2,1)S(1)} async-done(((bf16[16,128,512]{2,1,0:T(8,128)(2,1)}), bf16[16,128,512]{2,1,0:T(8,128)(2,1)S(1)}, u32[]{:S(2)}, u32[]{:S(2)}) %all-to-all-start.7) | async-done | bytes 2097184 | tf_op jit(solution)/shard_map/all_to_all | solution.py:319
  (58 shorter events, 79.2 us)
Async XLA Ops:
  7.2 111.5 %all-gather.3.cloned.1.call-start = ((), (), s32[]{:S(2)}) async-start(), calls=%async_computation.8 | async-start | bytes 4718592 | tf_op jit(solution)/shard_map/all_gather | solution.py:341
  45.7 5.5 %copy-start.2 = (bf16[1,2,2048,512]{3,2,1,0:T(8,128)(2,1)S(1)}, bf16[1,2,2048,512]{3,2,1,0:T(8,128)(2,1)}, u32[]{:S(2)}) copy-start(bf16[1,2,2048,512]{3,2,1,0:T(8,128)(2,1)} %old.7) | copy-start | bytes 12582916
  51.1 4.7 %copy-start.13 = (f32[1024,512]{1,0:T(8,128)}, f32[1024,512]{1,0:T(8,128)S(1)}, u32[]{:S(2)}) copy-start(f32[1024,512]{1,0:T(8,128)S(1)} %fusion.20) | copy-start | bytes 6291460
  55.8 31.0 %copy-start.1 = (bf16[1,128,2048]{2,1,0:T(8,128)(2,1)S(1)}, bf16[1,128,2048]{2,1,0:T(8,128)(2,1)}, u32[]{:S(2)}) copy-start(bf16[1,128,2048]{2,1,0:T(8,128)(2,1)} %param.9) | copy-start | bytes 1572868
  86.8 1.6 copy-start
  129.3 39.6 %all-to-all-start = ((bf16[16,128,512]{2,1,0:T(8,128)(2,1)}), bf16[16,128,512]{2,1,0:T(8,128)(2,1)}, u32[]{:S(2)}, u32[]{:S(2)}) async-start(bf16[16,128,512]{2,1,0:T(8,128)(2,1)} %bitcast.76), calls=%async_computation | async-start | bytes 4194304 | tf_op jit(solution)/shard_map/all_to_all | solution.py:319
  138.2 7.1 %copy-start.3 = (bf16[1,2,2048,512]{3,2,1,0:T(8,128)(2,1)S(1)}, bf16[1,2,2048,512]{3,2,1,0:T(8,128)(2,1)}, u32[]{:S(2)}) copy-start(bf16[1,2,2048,512]{3,2,1,0:T(8,128)(2,1)} %old.5) | copy-start | bytes 12582916
  145.2 4.4 %copy-start.10 = (bf16[8,128,2048]{2,1,0:T(8,128)(2,1)S(1)}, bf16[8,128,2048]{2,1,0:T(8,128)(2,1)}, u32[]{:S(2)}) copy-start(bf16[8,128,2048]{2,1,0:T(8,128)(2,1)} %gather.4) | copy-start | bytes 12582916
  168.9 5.2 %copy-start.12 = (s32[16,2]{0,1:T(2,128)S(1)}, s32[16,2]{0,1:T(2,128)}, u32[]{:S(2)}) copy-start(s32[16,2]{0,1:T(2,128)} %param.16) | copy-start | bytes 388
  168.9 47.8 %all-to-all-start.1 = ((bf16[16,128,512]{2,1,0:T(8,128)(2,1)}), bf16[16,128,512]{2,1,0:T(8,128)(2,1)}, u32[]{:S(2)}, u32[]{:S(2)}) async-start(bf16[16,128,512]{2,1,0:T(8,128)(2,1)} %bitcast.85), calls=%async_computation.1 | async-start | bytes 4194304 | tf_op jit(solution)/shard_map/all_to_all | solution.py:319
  202.0 12.5 %copy-start.4 = (f32[128,2048]{1,0:T(8,128)S(1)}, f32[128,2048]{1,0:T(8,128)}, u32[]{:S(2)}) copy-start(f32[128,2048]{1,0:T(8,128)} %scatter.3) | copy-start | bytes 3145732
  214.5 1.0 copy-start.11
  216.7 38.2 %all-to-all-start.2 = ((bf16[16,128,512]{2,1,0:T(8,128)(2,1)}), bf16[16,128,512]{2,1,0:T(8,128)(2,1)S(1)}, u32[]{:S(2)}, u32[]{:S(2)}) async-start(bf16[16,128,512]{2,1,0:T(8,128)(2,1)} %get-tuple-element.35), calls=%async_computation.2 | async-start | bytes 4194304 | tf_op jit(solution)/shard_map/all_to_all | solution.py:319
  255.0 7.5 %copy-start.5 = (bf16[16,128,512]{2,1,0:T(8,128)(2,1)}, bf16[16,128,512]{2,1,0:T(8,128)(2,1)S(1)}, u32[]{:S(2)}) copy-start(bf16[16,128,512]{2,1,0:T(8,128)(2,1)S(1)} %all-to-all-done.2) | copy-start | bytes 6291460
  262.4 32.5 %all-to-all-start.3 = ((bf16[16,128,512]{2,1,0:T(8,128)(2,1)}), bf16[16,128,512]{2,1,0:T(8,128)(2,1)S(1)}, u32[]{:S(2)}, u32[]{:S(2)}) async-start(bf16[16,128,512]{2,1,0:T(8,128)(2,1)} %bitcast.87), calls=%async_computation.3 | async-start | bytes 4194304 | tf_op jit(solution)/shard_map/all_to_all | solution.py:319
  266.3 7.1 %copy-start.9 = (bf16[8,128,2048]{2,1,0:T(8,128)(2,1)S(1)}, bf16[8,128,2048]{2,1,0:T(8,128)(2,1)}, u32[]{:S(2)}) copy-start(bf16[8,128,2048]{2,1,0:T(8,128)(2,1)} %gather.3) | copy-start | bytes 12582916
  295.0 1.3 copy-start.8
  296.3 31.5 %all-to-all-start.4 = ((bf16[16,128,512]{2,1,0:T(8,128)(2,1)}), bf16[16,128,512]{2,1,0:T(8,128)(2,1)}, u32[]{:S(2)}, u32[]{:S(2)}) async-start(bf16[16,128,512]{2,1,0:T(8,128)(2,1)} %bitcast.86), calls=%async_computation.4 | async-start | bytes 4194304 | tf_op jit(solution)/shard_map/all_to_all | solution.py:319
  327.8 29.9 %all-to-all-start.5 = ((bf16[16,128,512]{2,1,0:T(8,128)(2,1)}), bf16[16,128,512]{2,1,0:T(8,128)(2,1)S(1)}, u32[]{:S(2)}, u32[]{:S(2)}) async-start(bf16[16,128,512]{2,1,0:T(8,128)(2,1)} %get-tuple-element.44), calls=%async_computation.5 | async-start | bytes 4194304 | tf_op jit(solution)/shard_map/all_to_all | solution.py:319
  357.7 1.4 copy-start.6
  359.1 32.2 %all-to-all-start.6 = ((bf16[16,128,512]{2,1,0:T(8,128)(2,1)}), bf16[16,128,512]{2,1,0:T(8,128)(2,1)}, u32[]{:S(2)}, u32[]{:S(2)}) async-start(bf16[16,128,512]{2,1,0:T(8,128)(2,1)} %get-tuple-element.45), calls=%async_computation.6 | async-start | bytes 4194304 | tf_op jit(solution)/shard_map/all_to_all | solution.py:319
  391.3 32.0 %all-to-all-start.7 = ((bf16[16,128,512]{2,1,0:T(8,128)(2,1)}), bf16[16,128,512]{2,1,0:T(8,128)(2,1)S(1)}, u32[]{:S(2)}, u32[]{:S(2)}) async-start(bf16[16,128,512]{2,1,0:T(8,128)(2,1)} %get-tuple-element.46), calls=%async_computation.7 | async-start | bytes 4194304 | tf_op jit(solution)/shard_map/all_to_all | solution.py:319
  423.3 1.3 copy-start.7
Sparse Core Ops, SparseCore 0:
  9.7 43.1 all-gather.2
